TPU v7x, 512 devices: a whole 4x4x16 slice. The times are simulated.
512 devices in a mesh: dp: 16 (over z), expert: 32 (over y, x, core).
Axes of the slice: x: 4, y: 4, z: 16, core: 2. Of those that a mesh axis runs over, the one named last changes fastest.
Arguments:
- tokens: bfloat16 [2048, 4096], P('dp', 'expert'), may hold values from -6 to 6
- norm_gain: float32 [4096], replicated, may hold values from 0.1 to 1.9
- routes: int32 [2048, 2], P('dp'), may hold values from 0 to 31, all different within a row; in each aligned block of 128 rows (0 to 127, 128 to 255, ...) at most 10 rows name the same one
- route_prob: float32 [2048, 2], P('dp'), may hold values from 0.2 to 1
- gate_weight: bfloat16 [32, 4096, 2048], P('expert', None, 'dp'), may hold values from -0.09375 to 0.09375
- up_weight: bfloat16 [32, 4096, 2048], P('expert', None, 'dp'), may hold values from -0.09375 to 0.09375
- down_weight: bfloat16 [32, 2048, 4096], P('expert', 'dp'), may hold values from -0.125 to 0.125
- key_value_weight: bfloat16 [4096, 2048], P('expert'), may hold values from -0.09375 to 0.09375
- key_value_target: bfloat16 [2048, 2048], P('dp', 'expert'), may hold values from -6 to 6
- concept_mask: int32 [2048], P('dp'), may hold values 0 or 1
Outputs:
- down_grad: bfloat16 [32, 2048, 4096], P('expert', 'dp')
- key_value_grad: float32 [4096, 2048], P('expert', 'dp')
Inputs may be any that keep to these rules, and one draw needn't show every extreme that they name: `routes`: in each aligned block of 128 rows no expert is named by more than 10 rows; the two choices of a token differ.
All inputs are finite; a program needn't handle non-finite values. No bound on the sum of `concept_mask` on one device may be relied on, other than what follows from the above.
Results may differ from a plain program's by a relative error of at most 0.033.
Values may be sent and summed in bfloat16 or wider, within the bound.
No kernel may reach another device: no remote copies, remote signals or barrier semaphores. Data moves between devices by JAX's collectives and lax.ppermute only.
A program may use at most 64 MiB of HBM per device.

v0:
```python
import jax
import jax.numpy as jnp
from jax import lax
from jax.sharding import PartitionSpec as P

eps_norm = 1e-06


def slot_targets(routes, expert_count, capacity):
    flat = routes.reshape(-1)
    onehot = (flat[:, None] == jnp.arange(expert_count, dtype=jnp.int32)[None, :]).astype(jnp.int32)
    before = jnp.cumsum(onehot, axis=0) - onehot
    return flat * capacity + jnp.sum(before * onehot, axis=1)


def per_device(
    tokens,
    norm_gain,
    routes,
    route_prob,
    gate_weight,
    up_weight,
    down_weight,
    key_value_weight,
    key_value_target,
    concept_mask,
):
    token_rows, width = tokens.shape
    top_count = routes.shape[1]
    expert_count = lax.axis_size("expert")
    capacity = 5 * token_rows * top_count // (4 * expert_count)
    model_width = width * expert_count
    position = slot_targets(routes, expert_count, capacity)
    prob_flat = route_prob.reshape(-1)

    def place_rows(pair_rows):
        filled = (
            jnp.zeros((expert_count * capacity, width), jnp.bfloat16).at[position].set(pair_rows)
        )
        return filled.reshape(expert_count, capacity, width)

    values = tokens.astype(jnp.float32)
    total_sq = lax.psum(jnp.sum(values * values, axis=1), "expert")
    scale = lax.rsqrt(total_sq / model_width + eps_norm)
    local_gain = lax.dynamic_slice_in_dim(norm_gain, lax.axis_index("expert") * width, width)
    outgoing = (values * scale[:, None] * local_gain[None, :]).astype(jnp.bfloat16)
    send_slots = place_rows(jnp.repeat(outgoing, top_count, axis=0))
    arrived = lax.all_to_all(send_slots, "expert", split_axis=0, concat_axis=2, tiled=True)[0]
    rows = lax.all_gather(arrived, "dp", axis=0, tiled=True)
    gate_val = jnp.dot(rows, gate_weight[0], preferred_element_type=jnp.float32)
    up_val = jnp.dot(rows, up_weight[0], preferred_element_type=jnp.float32)
    hidden = (jax.nn.silu(gate_val) * up_val).astype(jnp.bfloat16)
    expert_out = lax.psum_scatter(
        jnp.dot(hidden, down_weight[0], preferred_element_type=jnp.float32).astype(jnp.bfloat16),
        "dp",
        scatter_dimension=0,
        tiled=True,
    )
    returned = lax.all_to_all(expert_out[None], "expert", split_axis=2, concat_axis=0, tiled=True)
    picked = returned.reshape(expert_count * capacity, width)[position].astype(jnp.float32)
    expert_mix = (picked * prob_flat[:, None]).reshape(token_rows, top_count, width).sum(axis=1)
    state = (tokens.astype(jnp.float32) + expert_mix).astype(jnp.bfloat16)
    proj_term = jnp.dot(state, key_value_weight, preferred_element_type=jnp.float32)
    proj_cols = lax.psum_scatter(
        proj_term.astype(jnp.bfloat16), "expert", scatter_dimension=1, tiled=True
    ).astype(jnp.float32)
    mask_col = concept_mask.astype(jnp.float32)[:, None]
    cotangent_cols = (
        mask_col * (proj_cols - key_value_target.astype(jnp.float32)) * token_rows ** (-0.5)
    ).astype(jnp.bfloat16)
    cotangent = lax.all_gather(cotangent_cols, "expert", axis=1, tiled=True)
    grad_term = jnp.einsum("tw,tk->wk", state, cotangent, preferred_element_type=jnp.float32)
    key_value_grad = lax.psum_scatter(
        grad_term.astype(jnp.bfloat16), "dp", scatter_dimension=1, tiled=True
    ).astype(jnp.float32)
    state_grad = jnp.einsum(
        "tk,wk->tw", cotangent, key_value_weight, preferred_element_type=jnp.float32
    )
    pair_grad = (jnp.repeat(state_grad, top_count, axis=0) * prob_flat[:, None]).astype(
        jnp.bfloat16
    )
    grad_slots = place_rows(pair_grad)
    landed = lax.all_to_all(grad_slots, "expert", split_axis=0, concat_axis=2, tiled=True)[0]
    down_total = jnp.einsum(
        "rf,rd->fd",
        hidden,
        lax.all_gather(landed, "dp", axis=0, tiled=True),
        preferred_element_type=jnp.float32,
    )
    return (down_total.astype(jnp.bfloat16)[None], key_value_grad)


def solution(mesh):
    placed = (
        P("dp", "expert"),
        P(),
        P("dp", None),
        P("dp", None),
        P("expert", None, "dp"),
        P("expert", None, "dp"),
        P("expert", "dp", None),
        P("expert", None),
        P("dp", "expert"),
        P("dp"),
    )
    return jax.shard_map(
        per_device,
        mesh=mesh,
        in_specs=placed,
        out_specs=(P("expert", "dp", None), P("expert", "dp")),
        check_vma=False,
    )
```

profile of v0, /device:TPU:2, one launch (start us, length us, event | category | flops | bytes accessed | tf_op | source)
XLA Modules:
  0.0 632.4 jit_solution(2933031377896465025)
XLA Ops:
  7.2 0.0 copy-start
  7.2 0.0 all-gather.5.cloned.1.call-start
  7.2 0.8 broadcast_multiply_fusion
  8.0 0.8 copy.34
  8.8 0.1 eq.29
  8.9 0.1 eq.25
  9.1 0.9 fusion.7
  9.9 63.0 %psum.7 = f32[128]{0:T(128)S(1)} all-reduce(f32[128]{0:T(128)S(1)} %fusion.7), channel_id=1, replica_groups=mesh['dp'=16,'expert'=32] {'expert'}, use_global_device_ids=true, to_apply=%region_4.5 | all-reduce | flops 128 | bytes 1024 | tf_op jit(solution)/shard_map/psum | solution.py:43
  72.9 0.1 copy.33
  73.0 0.1 mul.83
  73.2 0.6 reduce-window.6
  73.8 0.2 slice_reduce_fusion
  74.0 0.8 dynamic_slice.3
  74.8 0.8 fusion.9
  75.6 0.1 fusion.18
  75.8 1.2 scatter_custom_fusion
  77.0 14.9 %all_to_all.45 = bf16[32,10,128]{2,1,0:T(8,128)(2,1)S(1)} all-to-all(bf16[32,10,128]{2,1,0:T(8,128)(2,1)S(1)} %reshape.83), channel_id=1, replica_groups=mesh['dp'=16,'expert'=32] {'expert'}, dimensions={0} | all-to-all | bytes 163840 | tf_op jit(solution)/shard_map/all_to_all | solution.py:48
  92.0 0.7 reshape.112
  92.7 0.0 all-gather.5.cloned.1.call-update
  92.7 0.0 all-reduce.3.cloned.1.call-start
  92.8 74.1 %all-gather.5.cloned.1.call-done = bf16[16,10,4096]{2,1,0:T(8,128)(2,1)} async-done(((bf16[1,10,4096]{2,1,0:T(8,128)(2,1)}), bf16[16,10,4096]{2,1,0:T(8,128)(2,1)}) %all-gather.5.cloned.1.call-update) | async-done | bytes 1310736 | tf_op jit(solution)/shard_map/all_gather | solution.py:49
  166.9 1.8 reshape.113
  168.7 0.5 fusion.4
  169.2 0.7 copy-done.3
  170.0 0.5 fusion.1
  170.5 1.6 convolution_convert_fusion
  172.1 0.0 all-reduce.3.cloned.1.call-update
  172.1 0.1 copy.41
  172.2 1.3 dynamic-slice
  174.1 135.3 %all-reduce.3.cloned.1.call-done = bf16[160,4096]{1,0:T(8,128)(2,1)} async-done(((bf16[160,4096]{1,0:T(8,128)(2,1)}), bf16[160,4096]{1,0:T(8,128)(2,1)}) %all-reduce.3.cloned.1.call-update) | async-done | bytes 1310736
  309.4 1.0 dynamic-slice_bitcast_fusion
  310.4 2.8 copy.38
  313.2 0.5 broadcast.74
  313.7 23.4 %reduce.2 = bf16[4096,10]{1,0:T(8,128)(2,1)} reduce(bf16[4096,1,10]{2,1,0:T(2,128)(2,1)S(1)} %bitcast.74, bf16[]{:T(256)} %broadcast.74), dimensions={1}, to_apply=%bitcast.60.reduce_sub_computation | reduce | bytes 163842
  337.1 3.4 reshape.126
  340.5 7.4 %all-to-all-start.1 = ((bf16[32,2,640]{2,1,0:T(2,128)(2,1)}), bf16[32,2,640]{2,1,0:T(2,128)(2,1)S(1)}, u32[]{:S(2)}, u32[]{:S(2)}) async-start(bf16[32,2,640]{2,1,0:T(2,128)(2,1)} %reshape.126), calls=%async_computation.1 | async-start | bytes 163840 | tf_op jit(solution)/shard_map/all_to_all | solution.py:59
  348.0 0.0 reduce-scatter.5.cloned.1.call-start
  348.0 6.3 all-to-all-done.1
  354.3 2.2 reshape.127
  356.6 2.1 copy.39
  358.9 0.9 gather_fusion
  359.7 0.2 fusion.6
  360.0 1.1 convolution_convert_fusion.3
  361.1 0.0 reduce-scatter.5.cloned.1.call-update
  361.2 0.0 reduce-scatter.7.cloned.1.call-start
  361.2 93.7 %reduce-scatter.5.cloned.1.call-done = bf16[128,64]{0,1:T(8,128)(2,1)} async-done(((bf16[128,2048]{0,1:T(8,128)(2,1)}), bf16[128,64]{0,1:T(8,128)(2,1)}) %reduce-scatter.5.cloned.1.call-update) | async-done | bytes 16400 | tf_op jit(solution)/shard_map/reduce_scatter | solution.py:64
  455.0 0.7 multiply_convert_fusion.2
  455.7 23.2 %all_gather.10 = bf16[128,2048]{0,1:T(8,128)(2,1)S(1)} all-gather(bf16[128,64]{0,1:T(8,128)(2,1)S(1)} %multiply_convert_fusion.2), channel_id=1, replica_groups=mesh['dp'=16,'expert'=32] {'expert'}, dimensions={1}, use_global_device_ids=true | all-gather | bytes 540672 | tf_op jit(solution)/shard_map/all_gather | solution.py:71
  478.9 0.3 convolution_convert_fusion.2
  479.2 1.0 copy.44
  480.2 0.0 reduce-scatter.7.cloned.1.call-update
  480.2 0.0 all-gather.7.cloned.1.call-start
  480.3 0.1 mul.99
  480.4 0.3 fusion.22
  480.8 1.3 scatter_custom_fusion.1
  482.1 12.6 %all_to_all.46 = bf16[32,10,128]{2,1,0:T(8,128)(2,1)S(1)} all-to-all(bf16[32,10,128]{2,1,0:T(8,128)(2,1)S(1)} %reshape.86), channel_id=1, replica_groups=mesh['dp'=16,'expert'=32] {'expert'}, dimensions={0} | all-to-all | bytes 163840 | tf_op jit(solution)/shard_map/all_to_all | solution.py:83
  494.7 0.7 reshape.114
  495.4 0.0 all-gather.7.cloned.1.call-update
  495.4 54.2 %reduce-scatter.7.cloned.1.call-done = bf16[128,128]{1,0:T(8,128)(2,1)} async-done(((bf16[2048,128]{1,0:T(8,128)(2,1)}), bf16[128,128]{1,0:T(8,128)(2,1)}) %reduce-scatter.7.cloned.1.call-update) | async-done | bytes 32784
  549.6 0.9 copy.45
  550.5 0.6 convert_element_type.74
  551.1 71.5 %all-gather.7.cloned.1.call-done = bf16[16,10,4096]{2,1,0:T(8,128)(2,1)} async-done(((bf16[1,10,4096]{2,1,0:T(8,128)(2,1)}), bf16[16,10,4096]{2,1,0:T(8,128)(2,1)}) %all-gather.7.cloned.1.call-update) | async-done | bytes 1310736 | tf_op jit(solution)/shard_map/all_gather | solution.py:87
  622.7 1.8 reshape.115
  624.5 1.4 fusion
  (31 shorter events, 0.4 us)
Async XLA Ops:
  7.2 163.3 %copy-start = (bf16[1,128,4096]{2,1,0:T(8,128)(2,1)S(1)}, bf16[1,128,4096]{2,1,0:T(8,128)(2,1)}, u32[]{:S(2)}) copy-start(bf16[1,128,4096]{2,1,0:T(8,128)(2,1)} %param.16) | copy-start | bytes 3145732
  7.2 159.7 %all-gather.5.cloned.1.call-start = ((), (), s32[]{:S(2)}) async-start(), calls=%async_computation.6 | async-start | bytes 2228224 | tf_op jit(solution)/shard_map/all_gather | solution.py:49
  92.7 76.0 %copy-start.2 = (bf16[1,4096,128]{2,1,0:T(8,128)(2,1)S(1)}, bf16[1,4096,128]{2,1,0:T(8,128)(2,1)}, u32[]{:S(2)}) copy-start(bf16[1,4096,128]{2,1,0:T(8,128)(2,1)} %param.14) | copy-start | bytes 3145732
  92.7 216.7 %all-reduce.3.cloned.1.call-start = ((), (), s32[]{:S(2)}) async-start(), calls=%async_computation.9 | async-start | bytes 2621440
  168.7 1.2 copy-start.3
  170.5 1.6 copy-start.6
  340.5 13.8 %all-to-all-start.1 = ((bf16[32,2,640]{2,1,0:T(2,128)(2,1)}), bf16[32,2,640]{2,1,0:T(2,128)(2,1)S(1)}, u32[]{:S(2)}, u32[]{:S(2)}) async-start(bf16[32,2,640]{2,1,0:T(2,128)(2,1)} %reshape.126), calls=%async_computation.1 | async-start | bytes 163840 | tf_op jit(solution)/shard_map/all_to_all | solution.py:59
  348.0 107.0 %reduce-scatter.5.cloned.1.call-start = ((), (), s32[]{:S(2)}) async-start(), calls=%async_computation.5 | async-start | bytes 540672 | tf_op jit(solution)/shard_map/reduce_scatter | solution.py:64
  358.7 1.3 copy-start.1
  358.7 1.3 copy-start.4
  358.8 2.4 copy-start.7
  358.8 96.2 %copy-start.5 = (bf16[128,64]{0,1:T(8,128)(2,1)S(1)}, bf16[128,64]{0,1:T(8,128)(2,1)}, u32[]{:S(2)}) copy-start(bf16[128,64]{0,1:T(8,128)(2,1)} %param.18) | copy-start | bytes 49156
  361.2 188.5 %reduce-scatter.7.cloned.1.call-start = ((), (), s32[]{:S(2)}) async-start(), calls=%async_computation.8 | async-start | bytes 557056
  480.2 142.4 %all-gather.7.cloned.1.call-start = ((), (), s32[]{:S(2)}) async-start(), calls=%async_computation.7 | async-start | bytes 2228224 | tf_op jit(solution)/shard_map/all_gather | solution.py:87
Sparse Core Ops, SparseCore 0:
  92.8 74.0 all-gather.4
  172.2 137.1 all-reduce.2
  361.3 93.6 reduce-scatter.4
  480.3 69.2 reduce-scatter.6
  551.8 70.8 all-gather.6
where the time goes:
time: 633 us; the launch traced here: 632 us
  waiting for transfers between devices  435 us (69%)
  blocking collectives  114 us (18%)
  other arithmetic  29.5 us (5%)
  local copies, waits for them, and re-layouts  25.8 us (4%)
  between operations  14.8 us (2%)
  starting transfers between devices  7.63 us (1%)
    unnamed x7, waiting for transfers between devices  190 us
    reduce_scatter x1, waiting for transfers between devices, per_device(): lax.psum_scatter(proj_term.astype(jnp.bfloat16), 'expert', scatter_dimens...  93.7 us
    all_gather x1, waiting for transfers between devices, per_device(): rows = lax.all_gather(arrived, 'dp', axis=0, tiled=True)  74.1 us
    all_gather x1, waiting for transfers between devices, per_device(): lax.all_gather(landed, 'dp', axis=0, tiled=True)  71.5 us
    psum x1, blocking collectives, per_device(): total_sq = lax.psum(jnp.sum(values * values, axis=1), 'expert')  63 us
    unnamed x1, other arithmetic  23.4 us
    all_gather x1, blocking collectives, per_device(): cotangent = lax.all_gather(cotangent_cols, 'expert', axis=1, tiled=True)  23.2 us
    unnamed x29, local copies, waits for them, and re-layouts  16 us
  transfers between devices with their start and end apart: 6, of which 6 were waited for; matrix products, arithmetic and copies ran while one was open for 1% of the time, Pallas kernels for 0%

commit v1 on v0

--- a/solution.py
+++ b/solution.py
@@ -46,7 +46,12 @@
     outgoing = (values * scale[:, None] * local_gain[None, :]).astype(jnp.bfloat16)
     send_slots = place_rows(jnp.repeat(outgoing, top_count, axis=0))
     arrived = lax.all_to_all(send_slots, "expert", split_axis=0, concat_axis=2, tiled=True)[0]
-    rows = lax.all_gather(arrived, "dp", axis=0, tiled=True)
+    ring = [arrived]
+    for hop in range(15):
+        ring.append(lax.ppermute(ring[-1], "dp", [(dev, (dev + 1) % 16) for dev in range(16)]))
+    rows = jnp.roll(
+        jnp.concatenate(ring[::-1], axis=0), (lax.axis_index("dp") + 1) * ring[0].shape[0], axis=0
+    )
     gate_val = jnp.dot(rows, gate_weight[0], preferred_element_type=jnp.float32)
     up_val = jnp.dot(rows, up_weight[0], preferred_element_type=jnp.float32)
     hidden = (jax.nn.silu(gate_val) * up_val).astype(jnp.bfloat16)

time: 633 us -> 760 us (1.20)
  local copies, waits for them, and re-layouts: 25.8 us -> 92.6 us
  starting transfers between devices: 7.63 us -> 37.8 us
  waiting for transfers between devices: 435 us -> 459 us
    ppermute x0 -> x15, waiting for transfers between devices: none -> 99.6 us  [per_device(): lax.ppermute(ring[-1], 'dp', [(dev, (dev + 1) % 16) for dev in range(16)])]
    all_gather x1 -> x0, waiting for transfers between devices: 74.1 us -> none  [per_device(): rows = lax.all_gather(arrived, 'dp', axis=0, tiled=True)]
    concatenate x0 -> x1, local copies, waits for them, and re-layouts: none -> 67.9 us  [per_device(): jnp.roll(jnp.concatenate(ring[::-1], axis=0), (lax.axis_index('dp') + 1)...]
    ppermute x0 -> x15, starting transfers between devices: none -> 30 us  [per_device(): lax.ppermute(ring[-1], 'dp', [(dev, (dev + 1) % 16) for dev in range(16)])]
    unnamed x7 -> x6, waiting for transfers between devices: 190 us -> 188 us
    unnamed x29 -> x35, local copies, waits for them, and re-layouts: 16 us -> 14.9 us
  transfers between devices with their start and end apart: 6 -> 20, of which waited for: 6 -> 20; matrix products, arithmetic and copies ran while one was open for 1% -> 1% of each run, Pallas kernels for 0% -> 0%
where the time goes in v1:
time: 760 us; the launch traced here: 756 us
  waiting for transfers between devices  459 us (60%)
  blocking collectives  114 us (15%)
  local copies, waits for them, and re-layouts  92.6 us (12%)
  starting transfers between devices  37.8 us (5%)
  other arithmetic  29.4 us (4%)
  between operations  14.9 us (2%)
  matrix products  8.61 us (1%)
    unnamed x6, waiting for transfers between devices  188 us
    ppermute x15, waiting for transfers between devices, per_device(): lax.ppermute(ring[-1], 'dp', [(dev, (dev + 1) % 16) for dev in range(16)])  99.6 us
    reduce_scatter x1, waiting for transfers between devices, per_device(): lax.psum_scatter(proj_term.astype(jnp.bfloat16), 'expert', scatter_dimens...  93.7 us
    all_gather x1, waiting for transfers between devices, per_device(): lax.all_gather(landed, 'dp', axis=0, tiled=True)  71.6 us
    concatenate x1, local copies, waits for them, and re-layouts, per_device(): jnp.roll(jnp.concatenate(ring[::-1], axis=0), (lax.axis_index('dp') + 1)...  67.9 us
    psum x1, blocking collectives, per_device(): total_sq = lax.psum(jnp.sum(values * values, axis=1), 'expert')  63 us
    ppermute x15, starting transfers between devices, per_device(): lax.ppermute(ring[-1], 'dp', [(dev, (dev + 1) % 16) for dev in range(16)])  30 us
    unnamed x1, other arithmetic  23.4 us
  transfers between devices with their start and end apart: 20, of which 20 were waited for; matrix products, arithmetic and copies ran while one was open for 1% of the time, Pallas kernels for 0%

profile of v1, /device:TPU:2, one launch (start us, length us, event | category | flops | bytes accessed | tf_op | source)
XLA Modules:
  0.0 756.4 jit_solution(8119767465460582902)
XLA Ops:
  7.2 0.9 copy.34
  9.1 0.9 fusion.9
  9.9 63.0 %psum.7 = f32[128]{0:T(128)S(1)} all-reduce(f32[128]{0:T(128)S(1)} %fusion.9), channel_id=1, replica_groups=mesh['dp'=16,'expert'=32] {'expert'}, use_global_device_ids=true, to_apply=%region_4.5 | all-reduce | flops 128 | bytes 1024 | tf_op jit(solution)/shard_map/psum | solution.py:43
  74.0 0.8 dynamic_slice.7
  74.8 0.8 fusion.11
  75.8 1.2 scatter_custom_fusion
  77.0 14.9 %all_to_all.45 = bf16[32,10,128]{2,1,0:T(8,128)(2,1)S(1)} all-to-all(bf16[32,10,128]{2,1,0:T(8,128)(2,1)S(1)} %reshape.83), channel_id=1, replica_groups=mesh['dp'=16,'expert'=32] {'expert'}, dimensions={0} | all-to-all | bytes 163840 | tf_op jit(solution)/shard_map/all_to_all | solution.py:48
  92.1 3.1 collective-permute-start
  95.2 11.4 %collective-permute-done = bf16[10,4096]{1,0:T(8,128)(2,1)S(1)} collective-permute-done((bf16[10,4096]{1,0:T(8,128)(2,1)S(1)}, bf16[10,4096]{1,0:T(8,128)(2,1)S(1)}, u32[]{:S(2)}, u32[]{:S(2)}) %collective-permute-start) | collective-permute-done | bytes 81952 | tf_op jit(solution)/shard_map/ppermute | solution.py:51
  106.5 1.9 collective-permute-start.1
  108.5 6.2 collective-permute-done.1
  114.7 1.9 collective-permute-start.2
  116.6 6.1 collective-permute-done.2
  122.7 1.9 collective-permute-start.3
  124.7 6.1 collective-permute-done.3
  130.8 1.9 collective-permute-start.4
  132.7 6.1 collective-permute-done.4
  138.9 1.9 collective-permute-start.5
  140.8 6.3 collective-permute-done.5
  147.0 1.9 collective-permute-start.6
  149.0 7.4 collective-permute-done.6
  156.4 1.9 collective-permute-start.7
  158.3 6.7 collective-permute-done.7
  165.0 1.9 collective-permute-start.8
  166.9 6.1 collective-permute-done.8
  173.1 1.9 collective-permute-start.9
  175.0 6.1 collective-permute-done.9
  181.1 1.9 collective-permute-start.10
  183.0 6.1 collective-permute-done.10
  189.8 1.9 collective-permute-start.11
  191.8 6.1 collective-permute-done.11
  198.6 1.9 collective-permute-start.12
  200.5 6.1 collective-permute-done.12
  207.3 1.9 collective-permute-start.13
  209.2 6.2 collective-permute-done.13
  215.4 2.1 collective-permute-start.14
  217.6 6.2 collective-permute-done.14
  223.8 67.9 %concatenate.6 = bf16[320,4096]{1,0:T(8,128)(2,1)} concatenate(bf16[10,4096]{1,0:T(8,128)(2,1)} %collective-permute-done.14, bf16[10,4096]{1,0:T(8,128)(2,1)} %collective-permute-done.13, bf16[10,4096]{1,0:T(8,128)(2,1)} %copy-done.7, bf16[10,4096]{1,0:T(8,128)(2,1)} %copy-done.6, bf16[10,4096]{1,0:T(8,128)(2,1)} %copy-done.5, bf16[10,4096]{1,0:T(8,128)(2,1)S(1)} %collective-permute-done.9, ...), dimensions={0} | concatenate | bytes 5242880 | tf_op jit(solution)/shard_map/jit(_roll_dynamic)/concatenate | solution.py:52
  291.8 2.0 fusion.3
  293.7 1.9 multiply_convert_fusion.1
  295.6 1.6 convolution_convert_fusion
  297.3 1.3 dynamic-slice
  299.3 133.9 %all-reduce.3.cloned.1.call-done = bf16[160,4096]{1,0:T(8,128)(2,1)} async-done(((bf16[160,4096]{1,0:T(8,128)(2,1)}), bf16[160,4096]{1,0:T(8,128)(2,1)}) %all-reduce.3.cloned.1.call-update) | async-done | bytes 1310736
  433.2 1.0 dynamic-slice_bitcast_fusion
  434.2 2.8 copy.38
  437.5 23.4 %reduce.2 = bf16[4096,10]{1,0:T(8,128)(2,1)} reduce(bf16[4096,1,10]{2,1,0:T(2,128)(2,1)S(1)} %bitcast.76, bf16[]{:T(256)} %broadcast.74), dimensions={1}, to_apply=%bitcast.65.reduce_sub_computation | reduce | bytes 163842
  460.9 3.4 reshape.123
  464.3 7.6 %all-to-all-start.1 = ((bf16[32,2,640]{2,1,0:T(2,128)(2,1)}), bf16[32,2,640]{2,1,0:T(2,128)(2,1)S(1)}, u32[]{:S(2)}, u32[]{:S(2)}) async-start(bf16[32,2,640]{2,1,0:T(2,128)(2,1)} %reshape.123), calls=%async_computation.1 | async-start | bytes 163840 | tf_op jit(solution)/shard_map/all_to_all | solution.py:64
  472.0 6.3 all-to-all-done.1
  478.3 2.2 reshape.124
  480.6 2.1 copy.39
  482.9 0.9 gather_fusion
  484.0 1.1 convolution_convert_fusion.3
  485.2 93.7 %reduce-scatter.5.cloned.1.call-done = bf16[128,64]{0,1:T(8,128)(2,1)} async-done(((bf16[128,2048]{0,1:T(8,128)(2,1)}), bf16[128,64]{0,1:T(8,128)(2,1)}) %reduce-scatter.5.cloned.1.call-update) | async-done | bytes 16400 | tf_op jit(solution)/shard_map/reduce_scatter | solution.py:69
  579.0 0.7 multiply_convert_fusion.3
  579.7 23.1 %all_gather.6 = bf16[128,2048]{0,1:T(8,128)(2,1)S(1)} all-gather(bf16[128,64]{0,1:T(8,128)(2,1)S(1)} %multiply_convert_fusion.3), channel_id=1, replica_groups=mesh['dp'=16,'expert'=32] {'expert'}, dimensions={1}, use_global_device_ids=true | all-gather | bytes 540672 | tf_op jit(solution)/shard_map/all_gather | solution.py:76
  603.2 1.0 copy.44
  604.8 1.3 scatter_custom_fusion.1
  606.1 12.6 %all_to_all.46 = bf16[32,10,128]{2,1,0:T(8,128)(2,1)S(1)} all-to-all(bf16[32,10,128]{2,1,0:T(8,128)(2,1)S(1)} %reshape.86), channel_id=1, replica_groups=mesh['dp'=16,'expert'=32] {'expert'}, dimensions={0} | all-to-all | bytes 163840 | tf_op jit(solution)/shard_map/all_to_all | solution.py:88
  619.4 54.2 %reduce-scatter.7.cloned.1.call-done = bf16[128,128]{1,0:T(8,128)(2,1)} async-done(((bf16[2048,128]{1,0:T(8,128)(2,1)}), bf16[128,128]{1,0:T(8,128)(2,1)}) %reduce-scatter.7.cloned.1.call-update) | async-done | bytes 32784
  673.6 0.9 copy.45
  675.1 71.6 %all-gather.3.cloned.1.call-done = bf16[16,10,4096]{2,1,0:T(8,128)(2,1)} async-done(((bf16[1,10,4096]{2,1,0:T(8,128)(2,1)}), bf16[16,10,4096]{2,1,0:T(8,128)(2,1)}) %all-gather.3.cloned.1.call-update) | async-done | bytes 1310736 | tf_op jit(solution)/shard_map/all_gather | solution.py:92
  746.6 1.8 reshape.113
  748.4 1.4 fusion
  (65 shorter events, 7.8 us)
Async XLA Ops:
  7.2 288.4 %copy-start = (bf16[1,128,4096]{2,1,0:T(8,128)(2,1)S(1)}, bf16[1,128,4096]{2,1,0:T(8,128)(2,1)}, u32[]{:S(2)}) copy-start(bf16[1,128,4096]{2,1,0:T(8,128)(2,1)} %param.16) | copy-start | bytes 3145732
  7.2 426.0 %all-reduce.3.cloned.1.call-start = ((), (), s32[]{:S(2)}) async-start(), calls=%async_computation.8 | async-start | bytes 2621440
  92.1 14.5 %collective-permute-start = (bf16[10,4096]{1,0:T(8,128)(2,1)S(1)}, bf16[10,4096]{1,0:T(8,128)(2,1)S(1)}, u32[]{:S(2)}, u32[]{:S(2)}) collective-permute-start(bf16[10,4096]{1,0:T(8,128)(2,1)S(1)} %bitcast.79), channel_id=1, source_target_pairs={{0,32},{32,64},{64,96},{96,128},{128,160},{160,192},{192,224},{224... | collective-permute-start | bytes 245768 | tf_op jit(solution)/shard_map/ppermute | solution.py:51
  106.5 8.1 %collective-permute-start.1 = (bf16[10,4096]{1,0:T(8,128)(2,1)S(1)}, bf16[10,4096]{1,0:T(8,128)(2,1)S(1)}, u32[]{:S(2)}, u32[]{:S(2)}) collective-permute-start(bf16[10,4096]{1,0:T(8,128)(2,1)S(1)} %collective-permute-done), channel_id=1, source_target_pairs={{0,32},{32,64},{64,96},{96,128},{128,160},{160,192},{192,224},{224... | collective-permute-start | bytes 245768 | tf_op jit(solution)/shard_map/ppermute | solution.py:51
  114.7 8.1 %collective-permute-start.2 = (bf16[10,4096]{1,0:T(8,128)(2,1)S(1)}, bf16[10,4096]{1,0:T(8,128)(2,1)S(1)}, u32[]{:S(2)}, u32[]{:S(2)}) collective-permute-start(bf16[10,4096]{1,0:T(8,128)(2,1)S(1)} %collective-permute-done.1), channel_id=1, source_target_pairs={{0,32},{32,64},{64,96},{96,128},{128,160},{160,192},{192,224},{224... | collective-permute-start | bytes 245768 | tf_op jit(solution)/shard_map/ppermute | solution.py:51
  122.7 8.1 %collective-permute-start.3 = (bf16[10,4096]{1,0:T(8,128)(2,1)S(1)}, bf16[10,4096]{1,0:T(8,128)(2,1)S(1)}, u32[]{:S(2)}, u32[]{:S(2)}) collective-permute-start(bf16[10,4096]{1,0:T(8,128)(2,1)S(1)} %collective-permute-done.2), channel_id=1, source_target_pairs={{0,32},{32,64},{64,96},{96,128},{128,160},{160,192},{192,224},{224... | collective-permute-start | bytes 245768 | tf_op jit(solution)/shard_map/ppermute | solution.py:51
  130.8 8.1 %collective-permute-start.4 = (bf16[10,4096]{1,0:T(8,128)(2,1)S(1)}, bf16[10,4096]{1,0:T(8,128)(2,1)S(1)}, u32[]{:S(2)}, u32[]{:S(2)}) collective-permute-start(bf16[10,4096]{1,0:T(8,128)(2,1)S(1)} %collective-permute-done.3), channel_id=1, source_target_pairs={{0,32},{32,64},{64,96},{96,128},{128,160},{160,192},{192,224},{224... | collective-permute-start | bytes 245768 | tf_op jit(solution)/shard_map/ppermute | solution.py:51
  138.9 8.2 %collective-permute-start.5 = (bf16[10,4096]{1,0:T(8,128)(2,1)S(1)}, bf16[10,4096]{1,0:T(8,128)(2,1)S(1)}, u32[]{:S(2)}, u32[]{:S(2)}) collective-permute-start(bf16[10,4096]{1,0:T(8,128)(2,1)S(1)} %collective-permute-done.4), channel_id=1, source_target_pairs={{0,32},{32,64},{64,96},{96,128},{128,160},{160,192},{192,224},{224... | collective-permute-start | bytes 245768 | tf_op jit(solution)/shard_map/ppermute | solution.py:51
  147.0 9.3 %collective-permute-start.6 = (bf16[10,4096]{1,0:T(8,128)(2,1)S(1)}, bf16[10,4096]{1,0:T(8,128)(2,1)S(1)}, u32[]{:S(2)}, u32[]{:S(2)}) collective-permute-start(bf16[10,4096]{1,0:T(8,128)(2,1)S(1)} %collective-permute-done.5), channel_id=1, source_target_pairs={{0,32},{32,64},{64,96},{96,128},{128,160},{160,192},{192,224},{224... | collective-permute-start | bytes 245768 | tf_op jit(solution)/shard_map/ppermute | solution.py:51
  156.4 8.6 %collective-permute-start.7 = (bf16[10,4096]{1,0:T(8,128)(2,1)S(1)}, bf16[10,4096]{1,0:T(8,128)(2,1)S(1)}, u32[]{:S(2)}, u32[]{:S(2)}) collective-permute-start(bf16[10,4096]{1,0:T(8,128)(2,1)S(1)} %collective-permute-done.6), channel_id=1, source_target_pairs={{0,32},{32,64},{64,96},{96,128},{128,160},{160,192},{192,224},{224... | collective-permute-start | bytes 245768 | tf_op jit(solution)/shard_map/ppermute | solution.py:51
  165.0 8.1 %collective-permute-start.8 = (bf16[10,4096]{1,0:T(8,128)(2,1)S(1)}, bf16[10,4096]{1,0:T(8,128)(2,1)S(1)}, u32[]{:S(2)}, u32[]{:S(2)}) collective-permute-start(bf16[10,4096]{1,0:T(8,128)(2,1)S(1)} %collective-permute-done.7), channel_id=1, source_target_pairs={{0,32},{32,64},{64,96},{96,128},{128,160},{160,192},{192,224},{224... | collective-permute-start | bytes 245768 | tf_op jit(solution)/shard_map/ppermute | solution.py:51
  173.1 8.1 %collective-permute-start.9 = (bf16[10,4096]{1,0:T(8,128)(2,1)S(1)}, bf16[10,4096]{1,0:T(8,128)(2,1)S(1)}, u32[]{:S(2)}, u32[]{:S(2)}) collective-permute-start(bf16[10,4096]{1,0:T(8,128)(2,1)S(1)} %collective-permute-done.8), channel_id=1, source_target_pairs={{0,32},{32,64},{64,96},{96,128},{128,160},{160,192},{192,224},{224... | collective-permute-start | bytes 245768 | tf_op jit(solution)/shard_map/ppermute | solution.py:51
  181.1 8.1 %collective-permute-start.10 = (bf16[10,4096]{1,0:T(8,128)(2,1)S(1)}, bf16[10,4096]{1,0:T(8,128)(2,1)S(1)}, u32[]{:S(2)}, u32[]{:S(2)}) collective-permute-start(bf16[10,4096]{1,0:T(8,128)(2,1)S(1)} %collective-permute-done.9), channel_id=1, source_target_pairs={{0,32},{32,64},{64,96},{96,128},{128,160},{160,192},{192,224},{224... | collective-permute-start | bytes 245768 | tf_op jit(solution)/shard_map/ppermute | solution.py:51
  189.2 0.7 copy-start.5
  189.8 8.1 %collective-permute-start.11 = (bf16[10,4096]{1,0:T(8,128)(2,1)S(1)}, bf16[10,4096]{1,0:T(8,128)(2,1)S(1)}, u32[]{:S(2)}, u32[]{:S(2)}) collective-permute-start(bf16[10,4096]{1,0:T(8,128)(2,1)S(1)} %collective-permute-done.10), channel_id=1, source_target_pairs={{0,32},{32,64},{64,96},{96,128},{128,160},{160,192},{192,224},{224... | collective-permute-start | bytes 245768 | tf_op jit(solution)/shard_map/ppermute | solution.py:51
  197.9 0.7 copy-start.6
  198.6 8.1 %collective-permute-start.12 = (bf16[10,4096]{1,0:T(8,128)(2,1)S(1)}, bf16[10,4096]{1,0:T(8,128)(2,1)S(1)}, u32[]{:S(2)}, u32[]{:S(2)}) collective-permute-start(bf16[10,4096]{1,0:T(8,128)(2,1)S(1)} %collective-permute-done.11), channel_id=1, source_target_pairs={{0,32},{32,64},{64,96},{96,128},{128,160},{160,192},{192,224},{224... | collective-permute-start | bytes 245768 | tf_op jit(solution)/shard_map/ppermute | solution.py:51
  206.6 0.7 copy-start.7
  207.3 8.2 %collective-permute-start.13 = (bf16[10,4096]{1,0:T(8,128)(2,1)S(1)}, bf16[10,4096]{1,0:T(8,128)(2,1)}, u32[]{:S(2)}, u32[]{:S(2)}) collective-permute-start(bf16[10,4096]{1,0:T(8,128)(2,1)S(1)} %collective-permute-done.12), channel_id=1, source_target_pairs={{0,32},{32,64},{64,96},{96,128},{128,160},{160,192},{192,224},{224... | collective-permute-start | bytes 245768 | tf_op jit(solution)/shard_map/ppermute | solution.py:51
  215.4 8.4 %collective-permute-start.14 = (bf16[10,4096]{1,0:T(8,128)(2,1)}, bf16[10,4096]{1,0:T(8,128)(2,1)}, u32[]{:S(2)}, u32[]{:S(2)}) collective-permute-start(bf16[10,4096]{1,0:T(8,128)(2,1)} %collective-permute-done.13), channel_id=1, source_target_pairs={{0,32},{32,64},{64,96},{96,128},{128,160},{160,192},{192,224},{224... | collective-permute-start | bytes 245768 | tf_op jit(solution)/shard_map/ppermute | solution.py:51
  217.6 74.2 %copy-start.3 = (bf16[1,4096,128]{2,1,0:T(8,128)(2,1)S(1)}, bf16[1,4096,128]{2,1,0:T(8,128)(2,1)}, u32[]{:S(2)}) copy-start(bf16[1,4096,128]{2,1,0:T(8,128)(2,1)} %param.14) | copy-start | bytes 3145732
  291.7 2.0 copy-start.2
  295.6 1.6 copy-start.9
  464.3 14.0 %all-to-all-start.1 = ((bf16[32,2,640]{2,1,0:T(2,128)(2,1)}), bf16[32,2,640]{2,1,0:T(2,128)(2,1)S(1)}, u32[]{:S(2)}, u32[]{:S(2)}) async-start(bf16[32,2,640]{2,1,0:T(2,128)(2,1)} %reshape.123), calls=%async_computation.1 | async-start | bytes 163840 | tf_op jit(solution)/shard_map/all_to_all | solution.py:64
  472.0 107.0 %reduce-scatter.5.cloned.1.call-start = ((), (), s32[]{:S(2)}) async-start(), calls=%async_computation.5 | async-start | bytes 540672 | tf_op jit(solution)/shard_map/reduce_scatter | solution.py:69
  482.7 1.3 copy-start.1
  482.7 1.3 copy-start.4
  482.8 2.4 copy-start.10
  482.8 96.2 %copy-start.8 = (bf16[128,64]{0,1:T(8,128)(2,1)S(1)}, bf16[128,64]{0,1:T(8,128)(2,1)}, u32[]{:S(2)}) copy-start(bf16[128,64]{0,1:T(8,128)(2,1)} %param.18) | copy-start | bytes 49156
  485.2 188.4 %reduce-scatter.7.cloned.1.call-start = ((), (), s32[]{:S(2)}) async-start(), calls=%async_computation.7 | async-start | bytes 557056
  604.2 142.4 %all-gather.3.cloned.1.call-start = ((), (), s32[]{:S(2)}) async-start(), calls=%async_computation.6 | async-start | bytes 2228224 | tf_op jit(solution)/shard_map/all_gather | solution.py:92
Sparse Core Ops, SparseCore 0:
  297.3 135.8 all-reduce.2
  485.3 93.6 reduce-scatter.4
  604.3 69.2 reduce-scatter.6
  675.7 70.8 all-gather.2
